TPU v7x, 512 devices: a whole 4x4x16 slice. The times are simulated.
512 devices in a mesh: lon: 32 (over z, core), lat: 16 (over y, x).
Axes of the slice: x: 4, y: 4, z: 16, core: 2. Of those that a mesh axis runs over, the one named last changes fastest.
Arguments:
- perturbations: float32 [12, 3, 256, 4096], P(None, None, 'lat', 'lon'), as said below
- base_wind: float32 [2, 256, 4096], P(None, 'lat', 'lon'), may hold values from -4 to 4
- base_height: float32 [256, 4096], P('lat', 'lon'), may hold values from 0.5 to 1.5
Outputs:
- fields: float32 [12, 3, 256, 4096], P(None, None, 'lat', 'lon')
- factor: float32 [12, 12], replicated
Inputs may be any that keep to these rules, and one draw needn't show every extreme that they name: `perturbations`: finite real values.
All inputs are finite; a program needn't handle non-finite values.
Results may differ from a plain program's by a relative error of at most 0.00012.
Values sent between devices are 32-bit elements; how exact they have to be, the bound alone decides.
A program may use at most 64 MiB of HBM per device.

v0:
```python
import math
import jax
import jax.numpy as jnp
from jax import lax
from jax.sharding import PartitionSpec as P

STEPS = 8
advect_rate = 0.1
turn_rate = 0.5
gravity_rate = 0.2
diffuse_rate = 0.12


def with_halo(block, sides, width, periodic):
    for axis, dim in sides:
        count = lax.axis_size(axis)
        forward = [(i, i + 1) for i in range(count - 1)]
        if periodic:
            forward.append((count - 1, 0))
        backward = [(target, source) for source, target in forward]
        low = lax.ppermute(
            lax.slice_in_dim(block, block.shape[dim] - width, None, axis=dim), axis, forward
        )
        high = lax.ppermute(lax.slice_in_dim(block, 0, width, axis=dim), axis, backward)
        block = jnp.concatenate([low, block, high], axis=dim)
    return block


def centre(array):
    return array[..., 1:-1, 1:-1]


def diff_lon(array):
    return 0.5 * (array[..., 1:-1, 2:] - array[..., 1:-1, :-2])


def diff_lat(array):
    return 0.5 * (array[..., 2:, 1:-1] - array[..., :-2, 1:-1])


def laplacian(array):
    return (
        array[..., 2:, 1:-1]
        + array[..., :-2, 1:-1]
        + array[..., 1:-1, 2:]
        + array[..., 1:-1, :-2]
        - 4.0 * centre(array)
    )


def advance(field, base, turning):
    wind_x = field[..., 0, :, :]
    wind_y = field[..., 1, :, :]
    height = field[..., 2, :, :]
    base_x = base[0]
    base_y = base[1]
    base_depth = base[2]
    mean_x = centre(base_x)
    mean_y = centre(base_y)
    inner_x = centre(wind_x)
    inner_y = centre(wind_y)
    new_x = (
        inner_x
        - advect_rate
        * (
            mean_x * diff_lon(wind_x)
            + inner_x * diff_lon(base_x)
            + mean_y * diff_lat(wind_x)
            + inner_y * diff_lat(base_x)
        )
        + turn_rate * turning * inner_y
        - gravity_rate * diff_lon(height)
        + diffuse_rate * laplacian(wind_x)
    )
    new_y = (
        inner_y
        - advect_rate
        * (
            mean_x * diff_lon(wind_y)
            + inner_x * diff_lon(base_y)
            + mean_y * diff_lat(wind_y)
            + inner_y * diff_lat(base_y)
        )
        - turn_rate * turning * inner_x
        - gravity_rate * diff_lat(height)
        + diffuse_rate * laplacian(wind_y)
    )
    new_height = (
        centre(height)
        - advect_rate
        * (
            diff_lon(base_depth * wind_x + height * base_x)
            + diff_lat(base_depth * wind_y + height * base_y)
        )
        + diffuse_rate * laplacian(height)
    )
    return jnp.stack([new_x, new_y, new_height], axis=-3)


def coriolis(start, rows, total):
    glob = (start + jnp.arange(rows, dtype=jnp.int32)).astype(jnp.float32)
    return jnp.sin(math.pi * ((glob + 0.5) / total - 0.5))[:, None]


def inside_grid(start, rows, total):
    glob = start + jnp.arange(rows, dtype=jnp.int32)
    return ((glob >= 0) & (glob < total)).astype(jnp.float32)[:, None]


def extend(block, width):
    wide = with_halo(block, (("lon", 3),), width, True)
    return with_halo(wide, (("lat", 2),), width, False)


def per_device(perturbations, base_wind, base_height):
    rows = perturbations.shape[2]
    cols = perturbations.shape[3]
    total_rows = rows * lax.axis_size("lat")
    total_cols = cols * lax.axis_size("lon")
    row_start = lax.axis_index("lat") * rows
    depth = 2
    stacked = jnp.concatenate([base_wind, base_height[None]], axis=0)[None]
    base_ext = extend(stacked, depth)[0]
    field = perturbations
    for group_index in range(STEPS // depth):
        current = extend(field, depth)
        for inner_index in range(depth):
            margin = depth - 1 - inner_index
            turning = coriolis(row_start - margin, rows + 2 * margin, total_rows)
            base_margin = margin + 1
            current = advance(
                current,
                base_ext[
                    :,
                    depth - base_margin : depth + rows + base_margin,
                    depth - base_margin : depth + cols + base_margin,
                ],
                turning,
            )
            if margin > 0:
                current = current * inside_grid(row_start - margin, rows + 2 * margin, total_rows)
        field = current
    flattened = field.reshape(field.shape[0], -1)
    cell_count = float(3 * total_rows * total_cols)
    local_gram = jnp.dot(flattened, flattened.T, precision=lax.Precision.HIGHEST) / cell_count
    gram = lax.psum(local_gram, ("lon", "lat"))
    upper_factor = jnp.linalg.cholesky(gram).T
    lower_factor = upper_factor.T
    fields = jax.scipy.linalg.solve_triangular(lower_factor, flattened, lower=True)
    return (fields.reshape(perturbations.shape), upper_factor)


def solution(mesh):
    return jax.shard_map(
        per_device,
        mesh=mesh,
        in_specs=(P(None, None, "lat", "lon"), P(None, "lat", "lon"), P("lat", "lon")),
        out_specs=(P(None, None, "lat", "lon"), P()),
        check_vma=False,
    )
```

profile of v0, /device:TPU:1, one launch (start us, length us, event | category | flops | bytes accessed | tf_op | source)
XLA Modules:
  0.0 219.9 jit_solution(700765798616330664)
XLA Ops:
  0.6 0.7 maximum_bitcast_fusion
  1.4 3.0 %collective-permute-start.4 = (f32[1,3,16,2]{3,2,1,0:T(8,128)S(1)}, f32[1,3,16,2]{3,2,1,0:T(8,128)S(1)}, u32[]{:S(2)}, u32[]{:S(2)}) collective-permute-start(f32[1,3,16,2]{3,2,1,0:T(8,128)S(1)} %get-tuple-element.82), channel_id=1, source_target_pairs={{0,16},{16,32},{32,48},{48,64},{64,80},{80,96},{96,112},{112,128},... | collective-permute-start | bytes 1160 | tf_op jit(solution)/shard_map/ppermute | solution.py:21
  4.5 3.8 %collective-permute-start.5 = (f32[1,3,16,2]{3,2,1,0:T(8,128)S(1)}, f32[1,3,16,2]{3,2,1,0:T(8,128)S(1)}, u32[]{:S(2)}, u32[]{:S(2)}) collective-permute-start(f32[1,3,16,2]{3,2,1,0:T(8,128)S(1)} %get-tuple-element.83), channel_id=1, source_target_pairs={{16,0},{32,16},{48,32},{64,48},{80,64},{96,80},{112,96},{128,112},... | collective-permute-start | bytes 1160 | tf_op jit(solution)/shard_map/ppermute | solution.py:24
  8.3 1.1 copy.13
  9.6 3.6 %collective-permute-start.1 = (f32[12,3,16,2]{3,0,2,1:T(8,128)S(1)}, f32[12,3,16,2]{3,0,2,1:T(8,128)S(1)}, u32[]{:S(2)}, u32[]{:S(2)}) collective-permute-start(f32[12,3,16,2]{3,0,2,1:T(8,128)S(1)} %get-tuple-element.61), channel_id=1, source_target_pairs={{16,0},{32,16},{48,32},{64,48},{80,64},{96,80},{112,96},{128,112},... | collective-permute-start | bytes 13832 | tf_op jit(solution)/shard_map/ppermute | solution.py:24
  13.3 3.1 %collective-permute-start.6 = (f32[1,3,2,132]{3,2,1,0:T(2,128)S(1)}, f32[1,3,2,132]{3,2,1,0:T(2,128)S(1)}, u32[]{:S(2)}, u32[]{:S(2)}) collective-permute-start(f32[1,3,2,132]{3,2,1,0:T(2,128)S(1)} %get-tuple-element.68), channel_id=1, source_target_pairs={{0,1},{1,2},{2,3},{3,4},{4,5},{5,6},{6,7},{7,8},{8,9},{9,10},{10,1... | collective-permute-start | bytes 9512 | tf_op jit(solution)/shard_map/ppermute | solution.py:21
  16.5 1.3 collective-permute-start.7
  17.8 3.3 %collective-permute-done.7 = f32[1,3,2,132]{3,2,1,0:T(2,128)S(1)} collective-permute-done((f32[1,3,2,132]{3,2,1,0:T(2,128)S(1)}, f32[1,3,2,132]{3,2,1,0:T(2,128)S(1)}, u32[]{:S(2)}, u32[]{:S(2)}) %collective-permute-start.7) | collective-permute-done | bytes 3200 | tf_op jit(solution)/shard_map/ppermute | solution.py:24
  21.7 3.1 %collective-permute-start.2 = (f32[12,3,2,132]{3,0,2,1:T(8,128)S(1)}, f32[12,3,2,132]{3,0,2,1:T(8,128)S(1)}, u32[]{:S(2)}, u32[]{:S(2)}) collective-permute-start(f32[12,3,2,132]{3,0,2,1:T(8,128)S(1)} %get-tuple-element.12), channel_id=1, source_target_pairs={{0,1},{1,2},{2,3},{3,4},{4,5},{5,6},{6,7},{7,8},{8,9},{9,10},{10,1... | collective-permute-start | bytes 114056 | tf_op jit(solution)/shard_map/ppermute | solution.py:21
  24.9 1.3 collective-permute-start.3
  26.5 3.7 %collective-permute-done.3 = f32[12,3,2,132]{3,0,2,1:T(8,128)S(1)} collective-permute-done((f32[12,3,2,132]{3,0,2,1:T(8,128)S(1)}, f32[12,3,2,132]{3,0,2,1:T(8,128)S(1)}, u32[]{:S(2)}, u32[]{:S(2)}) %collective-permute-start.3) | collective-permute-done | bytes 38048 | tf_op jit(solution)/shard_map/ppermute | solution.py:24
  30.2 0.4 pad_maximum_fusion
  30.8 0.6 add_bitcast_fusion.7
  31.4 0.6 add_bitcast_fusion.6
  32.0 0.6 fusion.22
  33.3 0.3 add_bitcast_fusion.14
  33.6 0.3 fusion.42
  34.2 5.5 %collective-permute-start.9 = (f32[12,3,16,2]{3,0,2,1:T(8,128)S(1)}, f32[12,3,16,2]{3,0,2,1:T(8,128)S(1)}, u32[]{:S(2)}, u32[]{:S(2)}) collective-permute-start(f32[12,3,16,2]{3,0,2,1:T(8,128)S(1)} %get-tuple-element.59), channel_id=1, source_target_pairs={{16,0},{32,16},{48,32},{64,48},{80,64},{96,80},{112,96},{128,112},... | collective-permute-start | bytes 13832 | tf_op jit(solution)/shard_map/ppermute | solution.py:24
  39.7 1.2 collective-permute-done.8
  40.9 0.5 collective-permute-done.9
  41.5 4.7 %collective-permute-start.10 = (f32[12,3,2,132]{3,0,2,1:T(8,128)S(1)}, f32[12,3,2,132]{3,0,2,1:T(8,128)S(1)}, u32[]{:S(2)}, u32[]{:S(2)}) collective-permute-start(f32[12,3,2,132]{3,0,2,1:T(8,128)S(1)} %get-tuple-element.10), channel_id=1, source_target_pairs={{0,1},{1,2},{2,3},{3,4},{4,5},{5,6},{6,7},{7,8},{8,9},{9,10},{10,1... | collective-permute-start | bytes 114056 | tf_op jit(solution)/shard_map/ppermute | solution.py:21
  46.2 1.3 collective-permute-start.11
  47.5 0.3 collective-permute-done.10
  47.8 3.7 %collective-permute-done.11 = f32[12,3,2,132]{3,0,2,1:T(8,128)S(1)} collective-permute-done((f32[12,3,2,132]{3,0,2,1:T(8,128)S(1)}, f32[12,3,2,132]{3,0,2,1:T(8,128)S(1)}, u32[]{:S(2)}, u32[]{:S(2)}) %collective-permute-start.11) | collective-permute-done | bytes 38048 | tf_op jit(solution)/shard_map/ppermute | solution.py:24
  51.6 0.4 pad_maximum_fusion.1
  52.0 0.6 add_bitcast_fusion.5
  52.6 0.6 add_bitcast_fusion.4
  53.4 0.6 fusion.17
  54.5 0.3 add_bitcast_fusion.12
  55.0 0.3 fusion.37
  55.5 1.9 collective-permute-start.12
  57.4 6.0 %collective-permute-start.13 = (f32[12,3,16,2]{3,0,2,1:T(8,128)S(1)}, f32[12,3,16,2]{3,0,2,1:T(8,128)S(1)}, u32[]{:S(2)}, u32[]{:S(2)}) collective-permute-start(f32[12,3,16,2]{3,0,2,1:T(8,128)S(1)} %get-tuple-element.57), channel_id=1, source_target_pairs={{16,0},{32,16},{48,32},{64,48},{80,64},{96,80},{112,96},{128,112},... | collective-permute-start | bytes 13832 | tf_op jit(solution)/shard_map/ppermute | solution.py:24
  63.4 1.2 collective-permute-done.12
  64.9 3.8 %collective-permute-start.14 = (f32[12,3,2,132]{3,0,2,1:T(8,128)S(1)}, f32[12,3,2,132]{3,0,2,1:T(8,128)S(1)}, u32[]{:S(2)}, u32[]{:S(2)}) collective-permute-start(f32[12,3,2,132]{3,0,2,1:T(8,128)S(1)} %get-tuple-element.8), channel_id=1, source_target_pairs={{0,1},{1,2},{2,3},{3,4},{4,5},{5,6},{6,7},{7,8},{8,9},{9,10},{10,1... | collective-permute-start | bytes 114056 | tf_op jit(solution)/shard_map/ppermute | solution.py:21
  68.6 1.5 collective-permute-start.15
  70.2 4.0 %collective-permute-done.15 = f32[12,3,2,132]{3,0,2,1:T(8,128)S(1)} collective-permute-done((f32[12,3,2,132]{3,0,2,1:T(8,128)S(1)}, f32[12,3,2,132]{3,0,2,1:T(8,128)S(1)}, u32[]{:S(2)}, u32[]{:S(2)}) %collective-permute-start.15) | collective-permute-done | bytes 38048 | tf_op jit(solution)/shard_map/ppermute | solution.py:24
  74.3 0.4 pad_maximum_fusion.2
  74.7 0.6 add_bitcast_fusion.3
  75.3 0.6 add_bitcast_fusion.2
  76.1 0.6 fusion.12
  77.2 0.3 add_bitcast_fusion.10
  77.6 0.3 fusion.32
  78.2 1.0 collective-permute-start.16
  79.2 7.2 %collective-permute-start.17 = (f32[12,3,16,2]{3,0,2,1:T(8,128)S(1)}, f32[12,3,16,2]{3,0,2,1:T(8,128)S(1)}, u32[]{:S(2)}, u32[]{:S(2)}) collective-permute-start(f32[12,3,16,2]{3,0,2,1:T(8,128)S(1)} %get-tuple-element.55), channel_id=1, source_target_pairs={{16,0},{32,16},{48,32},{64,48},{80,64},{96,80},{112,96},{128,112},... | collective-permute-start | bytes 13832 | tf_op jit(solution)/shard_map/ppermute | solution.py:24
  86.4 1.2 collective-permute-done.16
  87.9 3.8 %collective-permute-start.18 = (f32[12,3,2,132]{3,0,2,1:T(8,128)S(1)}, f32[12,3,2,132]{3,0,2,1:T(8,128)S(1)}, u32[]{:S(2)}, u32[]{:S(2)}) collective-permute-start(f32[12,3,2,132]{3,0,2,1:T(8,128)S(1)} %get-tuple-element.6), channel_id=1, source_target_pairs={{0,1},{1,2},{2,3},{3,4},{4,5},{5,6},{6,7},{7,8},{8,9},{9,10},{10,1... | collective-permute-start | bytes 114056 | tf_op jit(solution)/shard_map/ppermute | solution.py:21
  91.7 1.3 collective-permute-start.19
  93.0 0.3 collective-permute-done.18
  93.3 4.0 %collective-permute-done.19 = f32[12,3,2,132]{3,0,2,1:T(8,128)S(1)} collective-permute-done((f32[12,3,2,132]{3,0,2,1:T(8,128)S(1)}, f32[12,3,2,132]{3,0,2,1:T(8,128)S(1)}, u32[]{:S(2)}, u32[]{:S(2)}) %collective-permute-start.19) | collective-permute-done | bytes 38048 | tf_op jit(solution)/shard_map/ppermute | solution.py:24
  97.3 0.4 pad_maximum_fusion.3
  97.7 0.6 add_bitcast_fusion.1
  98.3 0.6 add_bitcast_fusion
  99.1 0.6 fusion.7
  100.2 0.3 add_bitcast_fusion.8
  100.7 0.3 fusion.27
  101.0 0.6 fusion
  101.7 112.7 %psum.7 = f32[12,12]{0,1:T(8,128)S(1)} all-reduce(f32[12,12]{0,1:T(8,128)S(1)} %fusion), channel_id=1, replica_groups=mesh['lon'=32,'lat'=16] {'lon','lat'}, use_global_device_ids=true, to_apply=%region_0.0 | all-reduce | flops 144 | bytes 1152 | tf_op jit(solution)/shard_map/psum | solution.py:146
  214.4 1.1 cholesky.16
  215.5 0.6 compare_reduce_fusion
  216.2 0.6 fusion.53
  216.9 0.9 custom-call.7
  217.9 0.5 fusion.1
  218.4 0.8 copy.21
  219.2 0.7 copy.22
  (62 shorter events, 6.4 us)
Async XLA Ops:
  1.4 11.8 %collective-permute-start.4 = (f32[1,3,16,2]{3,2,1,0:T(8,128)S(1)}, f32[1,3,16,2]{3,2,1,0:T(8,128)S(1)}, u32[]{:S(2)}, u32[]{:S(2)}) collective-permute-start(f32[1,3,16,2]{3,2,1,0:T(8,128)S(1)} %get-tuple-element.82), channel_id=1, source_target_pairs={{0,16},{16,32},{32,48},{48,64},{64,80},{80,96},{96,112},{112,128},... | collective-permute-start | bytes 1160 | tf_op jit(solution)/shard_map/ppermute | solution.py:21
  4.5 8.8 %collective-permute-start.5 = (f32[1,3,16,2]{3,2,1,0:T(8,128)S(1)}, f32[1,3,16,2]{3,2,1,0:T(8,128)S(1)}, u32[]{:S(2)}, u32[]{:S(2)}) collective-permute-start(f32[1,3,16,2]{3,2,1,0:T(8,128)S(1)} %get-tuple-element.83), channel_id=1, source_target_pairs={{16,0},{32,16},{48,32},{64,48},{80,64},{96,80},{112,96},{128,112},... | collective-permute-start | bytes 1160 | tf_op jit(solution)/shard_map/ppermute | solution.py:24
  9.5 12.0 %collective-permute-start = (f32[12,3,16,2]{3,0,2,1:T(8,128)S(1)}, f32[12,3,16,2]{3,0,2,1:T(8,128)S(1)}, u32[]{:S(2)}, u32[]{:S(2)}) collective-permute-start(f32[12,3,16,2]{3,0,2,1:T(8,128)S(1)} %get-tuple-element.60), channel_id=1, source_target_pairs={{0,16},{16,32},{32,48},{48,64},{64,80},{80,96},{96,112},{112,128},... | collective-permute-start | bytes 13832 | tf_op jit(solution)/shard_map/ppermute | solution.py:21
  9.6 12.0 %collective-permute-start.1 = (f32[12,3,16,2]{3,0,2,1:T(8,128)S(1)}, f32[12,3,16,2]{3,0,2,1:T(8,128)S(1)}, u32[]{:S(2)}, u32[]{:S(2)}) collective-permute-start(f32[12,3,16,2]{3,0,2,1:T(8,128)S(1)} %get-tuple-element.61), channel_id=1, source_target_pairs={{16,0},{32,16},{48,32},{64,48},{80,64},{96,80},{112,96},{128,112},... | collective-permute-start | bytes 13832 | tf_op jit(solution)/shard_map/ppermute | solution.py:24
  13.3 4.5 %collective-permute-start.6 = (f32[1,3,2,132]{3,2,1,0:T(2,128)S(1)}, f32[1,3,2,132]{3,2,1,0:T(2,128)S(1)}, u32[]{:S(2)}, u32[]{:S(2)}) collective-permute-start(f32[1,3,2,132]{3,2,1,0:T(2,128)S(1)} %get-tuple-element.68), channel_id=1, source_target_pairs={{0,1},{1,2},{2,3},{3,4},{4,5},{5,6},{6,7},{7,8},{8,9},{9,10},{10,1... | collective-permute-start | bytes 9512 | tf_op jit(solution)/shard_map/ppermute | solution.py:21
  16.5 4.7 %collective-permute-start.7 = (f32[1,3,2,132]{3,2,1,0:T(2,128)S(1)}, f32[1,3,2,132]{3,2,1,0:T(2,128)S(1)}, u32[]{:S(2)}, u32[]{:S(2)}) collective-permute-start(f32[1,3,2,132]{3,2,1,0:T(2,128)S(1)} %get-tuple-element.69), channel_id=1, source_target_pairs={{1,0},{2,1},{3,2},{4,3},{5,4},{6,5},{7,6},{8,7},{9,8},{10,9},{11,1... | collective-permute-start | bytes 9512 | tf_op jit(solution)/shard_map/ppermute | solution.py:24
  21.7 4.7 %collective-permute-start.2 = (f32[12,3,2,132]{3,0,2,1:T(8,128)S(1)}, f32[12,3,2,132]{3,0,2,1:T(8,128)S(1)}, u32[]{:S(2)}, u32[]{:S(2)}) collective-permute-start(f32[12,3,2,132]{3,0,2,1:T(8,128)S(1)} %get-tuple-element.12), channel_id=1, source_target_pairs={{0,1},{1,2},{2,3},{3,4},{4,5},{5,6},{6,7},{7,8},{8,9},{9,10},{10,1... | collective-permute-start | bytes 114056 | tf_op jit(solution)/shard_map/ppermute | solution.py:21
  24.9 5.4 %collective-permute-start.3 = (f32[12,3,2,132]{3,0,2,1:T(8,128)S(1)}, f32[12,3,2,132]{3,0,2,1:T(8,128)S(1)}, u32[]{:S(2)}, u32[]{:S(2)}) collective-permute-start(f32[12,3,2,132]{3,0,2,1:T(8,128)S(1)} %get-tuple-element.13), channel_id=1, source_target_pairs={{1,0},{2,1},{3,2},{4,3},{5,4},{6,5},{7,6},{8,7},{9,8},{10,9},{11,1... | collective-permute-start | bytes 114056 | tf_op jit(solution)/shard_map/ppermute | solution.py:24
  34.1 6.7 %collective-permute-start.8 = (f32[12,3,16,2]{3,0,2,1:T(8,128)S(1)}, f32[12,3,16,2]{3,0,2,1:T(8,128)S(1)}, u32[]{:S(2)}, u32[]{:S(2)}) collective-permute-start(f32[12,3,16,2]{3,0,2,1:T(8,128)S(1)} %get-tuple-element.58), channel_id=1, source_target_pairs={{0,16},{16,32},{32,48},{48,64},{64,80},{80,96},{96,112},{112,128},... | collective-permute-start | bytes 13832 | tf_op jit(solution)/shard_map/ppermute | solution.py:21
  34.2 7.2 %collective-permute-start.9 = (f32[12,3,16,2]{3,0,2,1:T(8,128)S(1)}, f32[12,3,16,2]{3,0,2,1:T(8,128)S(1)}, u32[]{:S(2)}, u32[]{:S(2)}) collective-permute-start(f32[12,3,16,2]{3,0,2,1:T(8,128)S(1)} %get-tuple-element.59), channel_id=1, source_target_pairs={{16,0},{32,16},{48,32},{64,48},{80,64},{96,80},{112,96},{128,112},... | collective-permute-start | bytes 13832 | tf_op jit(solution)/shard_map/ppermute | solution.py:24
  41.5 6.3 %collective-permute-start.10 = (f32[12,3,2,132]{3,0,2,1:T(8,128)S(1)}, f32[12,3,2,132]{3,0,2,1:T(8,128)S(1)}, u32[]{:S(2)}, u32[]{:S(2)}) collective-permute-start(f32[12,3,2,132]{3,0,2,1:T(8,128)S(1)} %get-tuple-element.10), channel_id=1, source_target_pairs={{0,1},{1,2},{2,3},{3,4},{4,5},{5,6},{6,7},{7,8},{8,9},{9,10},{10,1... | collective-permute-start | bytes 114056 | tf_op jit(solution)/shard_map/ppermute | solution.py:21
  46.2 5.4 %collective-permute-start.11 = (f32[12,3,2,132]{3,0,2,1:T(8,128)S(1)}, f32[12,3,2,132]{3,0,2,1:T(8,128)S(1)}, u32[]{:S(2)}, u32[]{:S(2)}) collective-permute-start(f32[12,3,2,132]{3,0,2,1:T(8,128)S(1)} %get-tuple-element.11), channel_id=1, source_target_pairs={{1,0},{2,1},{3,2},{4,3},{5,4},{6,5},{7,6},{8,7},{9,8},{10,9},{11,1... | collective-permute-start | bytes 114056 | tf_op jit(solution)/shard_map/ppermute | solution.py:24
  55.5 9.1 %collective-permute-start.12 = (f32[12,3,16,2]{3,0,2,1:T(8,128)S(1)}, f32[12,3,16,2]{3,0,2,1:T(8,128)S(1)}, u32[]{:S(2)}, u32[]{:S(2)}) collective-permute-start(f32[12,3,16,2]{3,0,2,1:T(8,128)S(1)} %get-tuple-element.56), channel_id=1, source_target_pairs={{0,16},{16,32},{32,48},{48,64},{64,80},{80,96},{96,112},{112,128},... | collective-permute-start | bytes 13832 | tf_op jit(solution)/shard_map/ppermute | solution.py:21
  57.4 7.4 %collective-permute-start.13 = (f32[12,3,16,2]{3,0,2,1:T(8,128)S(1)}, f32[12,3,16,2]{3,0,2,1:T(8,128)S(1)}, u32[]{:S(2)}, u32[]{:S(2)}) collective-permute-start(f32[12,3,16,2]{3,0,2,1:T(8,128)S(1)} %get-tuple-element.57), channel_id=1, source_target_pairs={{16,0},{32,16},{48,32},{64,48},{80,64},{96,80},{112,96},{128,112},... | collective-permute-start | bytes 13832 | tf_op jit(solution)/shard_map/ppermute | solution.py:24
  64.9 5.4 %collective-permute-start.14 = (f32[12,3,2,132]{3,0,2,1:T(8,128)S(1)}, f32[12,3,2,132]{3,0,2,1:T(8,128)S(1)}, u32[]{:S(2)}, u32[]{:S(2)}) collective-permute-start(f32[12,3,2,132]{3,0,2,1:T(8,128)S(1)} %get-tuple-element.8), channel_id=1, source_target_pairs={{0,1},{1,2},{2,3},{3,4},{4,5},{5,6},{6,7},{7,8},{8,9},{9,10},{10,1... | collective-permute-start | bytes 114056 | tf_op jit(solution)/shard_map/ppermute | solution.py:21
  68.6 5.6 %collective-permute-start.15 = (f32[12,3,2,132]{3,0,2,1:T(8,128)S(1)}, f32[12,3,2,132]{3,0,2,1:T(8,128)S(1)}, u32[]{:S(2)}, u32[]{:S(2)}) collective-permute-start(f32[12,3,2,132]{3,0,2,1:T(8,128)S(1)} %get-tuple-element.9), channel_id=1, source_target_pairs={{1,0},{2,1},{3,2},{4,3},{5,4},{6,5},{7,6},{8,7},{9,8},{10,9},{11,1... | collective-permute-start | bytes 114056 | tf_op jit(solution)/shard_map/ppermute | solution.py:24
  78.2 9.4 %collective-permute-start.16 = (f32[12,3,16,2]{3,0,2,1:T(8,128)S(1)}, f32[12,3,16,2]{3,0,2,1:T(8,128)S(1)}, u32[]{:S(2)}, u32[]{:S(2)}) collective-permute-start(f32[12,3,16,2]{3,0,2,1:T(8,128)S(1)} %get-tuple-element.54), channel_id=1, source_target_pairs={{0,16},{16,32},{32,48},{48,64},{64,80},{80,96},{96,112},{112,128},... | collective-permute-start | bytes 13832 | tf_op jit(solution)/shard_map/ppermute | solution.py:21
  79.2 8.6 %collective-permute-start.17 = (f32[12,3,16,2]{3,0,2,1:T(8,128)S(1)}, f32[12,3,16,2]{3,0,2,1:T(8,128)S(1)}, u32[]{:S(2)}, u32[]{:S(2)}) collective-permute-start(f32[12,3,16,2]{3,0,2,1:T(8,128)S(1)} %get-tuple-element.55), channel_id=1, source_target_pairs={{16,0},{32,16},{48,32},{64,48},{80,64},{96,80},{112,96},{128,112},... | collective-permute-start | bytes 13832 | tf_op jit(solution)/shard_map/ppermute | solution.py:24
  87.9 5.4 %collective-permute-start.18 = (f32[12,3,2,132]{3,0,2,1:T(8,128)S(1)}, f32[12,3,2,132]{3,0,2,1:T(8,128)S(1)}, u32[]{:S(2)}, u32[]{:S(2)}) collective-permute-start(f32[12,3,2,132]{3,0,2,1:T(8,128)S(1)} %get-tuple-element.6), channel_id=1, source_target_pairs={{0,1},{1,2},{2,3},{3,4},{4,5},{5,6},{6,7},{7,8},{8,9},{9,10},{10,1... | collective-permute-start | bytes 114056 | tf_op jit(solution)/shard_map/ppermute | solution.py:21
  91.7 5.6 %collective-permute-start.19 = (f32[12,3,2,132]{3,0,2,1:T(8,128)S(1)}, f32[12,3,2,132]{3,0,2,1:T(8,128)S(1)}, u32[]{:S(2)}, u32[]{:S(2)}) collective-permute-start(f32[12,3,2,132]{3,0,2,1:T(8,128)S(1)} %get-tuple-element.7), channel_id=1, source_target_pairs={{1,0},{2,1},{3,2},{4,3},{5,4},{6,5},{7,6},{8,7},{9,8},{10,9},{11,1... | collective-permute-start | bytes 114056 | tf_op jit(solution)/shard_map/ppermute | solution.py:24
where the time goes:
time: 221 us; the launch traced here: 220 us
  blocking collectives  113 us (51%)
  starting transfers between devices  57.2 us (26%)
  waiting for transfers between devices  24.3 us (11%)
  other arithmetic  19.3 us (9%)
  local copies, waits for them, and re-layouts  4.13 us (2%)
    psum x1, blocking collectives, per_device(): gram = lax.psum(local_gram, ('lon', 'lat'))  113 us
    ppermute x10, starting transfers between devices, with_halo(): lax.ppermute(lax.slice_in_dim(block, 0, width, axis=dim), axis, backward)  32.8 us
    ppermute x10, starting transfers between devices, with_halo(): lax.ppermute(lax.slice_in_dim(block, block.shape[dim] - width, None, axis...  24.4 us
    ppermute x10, waiting for transfers between devices, with_halo(): lax.ppermute(lax.slice_in_dim(block, 0, width, axis=dim), axis, backward)  19.7 us
    another operation x28, other arithmetic, advance(): return jnp.stack([new_x, new_y, new_height], axis=-3)  11 us
    ppermute x10, waiting for transfers between devices, with_halo(): lax.ppermute(lax.slice_in_dim(block, block.shape[dim] - width, None, axis...  4.58 us
  transfers between devices with their start and end apart: 20, of which 15 were waited for; matrix products, arithmetic and copies ran while one was open for 1% of the time, Pallas kernels for 0%

commit v1 on v0

--- a/solution.py
+++ b/solution.py
@@ -1,14 +1,23 @@
+import functools
 import math
 import jax
 import jax.numpy as jnp
 from jax import lax
 from jax.sharding import PartitionSpec as P
+from jax.lax import all_gather
 
 STEPS = 8
 advect_rate = 0.1
 turn_rate = 0.5
 gravity_rate = 0.2
 diffuse_rate = 0.12
+
+
+def _render_local_data(xin, chip_axis):
+    return all_gather(xin, chip_axis).sum(axis=0)
+
+
+joints_remake = functools.partial(_render_local_data, chip_axis=("lon", "lat"))
 
 
 def with_halo(block, sides, width, periodic):
@@ -143,7 +152,7 @@
     flattened = field.reshape(field.shape[0], -1)
     cell_count = float(3 * total_rows * total_cols)
     local_gram = jnp.dot(flattened, flattened.T, precision=lax.Precision.HIGHEST) / cell_count
-    gram = lax.psum(local_gram, ("lon", "lat"))
+    gram = joints_remake(local_gram)
     upper_factor = jnp.linalg.cholesky(gram).T
     lower_factor = upper_factor.T
     fields = jax.scipy.linalg.solve_triangular(lower_factor, flattened, lower=True)

time: 221 us -> 372 us (1.68)
  blocking collectives: 113 us -> 261 us
    all_gather x0 -> x1, blocking collectives: none -> 261 us  [_render_local_data(): return all_gather(xin, chip_axis).sum(axis=0)]
    psum x1 -> x0, blocking collectives: 113 us -> none  [per_device(): gram = lax.psum(local_gram, ('lon', 'lat'))]
where the time goes in v1:
time: 372 us; the launch traced here: 371 us
  blocking collectives  261 us (70%)
  starting transfers between devices  57.2 us (15%)
  waiting for transfers between devices  24.3 us (7%)
  other arithmetic  22.1 us (6%)
  local copies, waits for them, and re-layouts  4.13 us (1%)
    all_gather x1, blocking collectives, _render_local_data(): return all_gather(xin, chip_axis).sum(axis=0)  261 us
    ppermute x10, starting transfers between devices, with_halo(): lax.ppermute(lax.slice_in_dim(block, 0, width, axis=dim), axis, backward)  32.8 us
    ppermute x10, starting transfers between devices, with_halo(): lax.ppermute(lax.slice_in_dim(block, block.shape[dim] - width, None, axis...  24.4 us
    ppermute x10, waiting for transfers between devices, with_halo(): lax.ppermute(lax.slice_in_dim(block, 0, width, axis=dim), axis, backward)  19.7 us
    another operation x28, other arithmetic, advance(): return jnp.stack([new_x, new_y, new_height], axis=-3)  11 us
  transfers between devices with their start and end apart: 20, of which 15 were waited for; matrix products, arithmetic and copies ran while one was open for 1% of the time, Pallas kernels for 0%

profile of v1, /device:TPU:1, one launch (start us, length us, event | category | flops | bytes accessed | tf_op | source)
XLA Modules:
  0.0 371.2 jit_solution(12724543776136655561)
XLA Ops:
  0.6 0.7 maximum_bitcast_fusion
  1.4 3.0 collective-permute-start.4
  4.5 3.8 %collective-permute-start.5 = (f32[1,3,16,2]{3,2,1,0:T(8,128)S(1)}, f32[1,3,16,2]{3,2,1,0:T(8,128)S(1)}, u32[]{:S(2)}, u32[]{:S(2)}) collective-permute-start(f32[1,3,16,2]{3,2,1,0:T(8,128)S(1)} %get-tuple-element.85), channel_id=1, source_target_pairs={{16,0},{32,16},{48,32},{64,48},{80,64},{96,80},{112,96},{128,112},... | collective-permute-start | bytes 1160 | tf_op jit(solution)/shard_map/ppermute | solution.py:33
  8.3 1.1 copy.21
  9.6 3.6 collective-permute-start.1
  13.4 3.1 collective-permute-start.6
  16.5 1.3 collective-permute-start.7
  17.8 3.3 collective-permute-done.7
  21.7 3.1 collective-permute-start.2
  24.9 1.3 collective-permute-start.3
  26.5 3.7 %collective-permute-done.3 = f32[12,3,2,132]{3,0,2,1:T(8,128)S(1)} collective-permute-done((f32[12,3,2,132]{3,0,2,1:T(8,128)S(1)}, f32[12,3,2,132]{3,0,2,1:T(8,128)S(1)}, u32[]{:S(2)}, u32[]{:S(2)}) %collective-permute-start.3) | collective-permute-done | bytes 38048 | tf_op jit(solution)/shard_map/ppermute | solution.py:33
  30.2 0.4 pad_maximum_fusion
  30.8 0.6 fusion.23
  31.5 0.6 add_bitcast_fusion.7
  32.0 0.6 add_bitcast_fusion.6
  33.0 0.3 fusion.43
  33.6 0.3 add_bitcast_fusion.14
  34.2 5.5 %collective-permute-start.9 = (f32[12,3,16,2]{3,0,2,1:T(8,128)S(1)}, f32[12,3,16,2]{3,0,2,1:T(8,128)S(1)}, u32[]{:S(2)}, u32[]{:S(2)}) collective-permute-start(f32[12,3,16,2]{3,0,2,1:T(8,128)S(1)} %get-tuple-element.61), channel_id=1, source_target_pairs={{16,0},{32,16},{48,32},{64,48},{80,64},{96,80},{112,96},{128,112},... | collective-permute-start | bytes 13832 | tf_op jit(solution)/shard_map/ppermute | solution.py:33
  39.7 1.2 collective-permute-done.8
  40.9 0.5 collective-permute-done.9
  41.5 4.7 %collective-permute-start.10 = (f32[12,3,2,132]{3,0,2,1:T(8,128)S(1)}, f32[12,3,2,132]{3,0,2,1:T(8,128)S(1)}, u32[]{:S(2)}, u32[]{:S(2)}) collective-permute-start(f32[12,3,2,132]{3,0,2,1:T(8,128)S(1)} %get-tuple-element.12), channel_id=1, source_target_pairs={{0,1},{1,2},{2,3},{3,4},{4,5},{5,6},{6,7},{7,8},{8,9},{9,10},{10,1... | collective-permute-start | bytes 114056 | tf_op jit(solution)/shard_map/ppermute | solution.py:30
  46.3 1.3 collective-permute-start.11
  47.6 0.3 collective-permute-done.10
  47.9 3.7 %collective-permute-done.11 = f32[12,3,2,132]{3,0,2,1:T(8,128)S(1)} collective-permute-done((f32[12,3,2,132]{3,0,2,1:T(8,128)S(1)}, f32[12,3,2,132]{3,0,2,1:T(8,128)S(1)}, u32[]{:S(2)}, u32[]{:S(2)}) %collective-permute-start.11) | collective-permute-done | bytes 38048 | tf_op jit(solution)/shard_map/ppermute | solution.py:33
  51.6 0.4 pad_maximum_fusion.1
  52.2 0.6 add_bitcast_fusion.5
  52.8 0.6 add_bitcast_fusion.4
  53.4 0.6 fusion.18
  54.7 0.3 add_bitcast_fusion.12
  55.0 0.3 fusion.38
  55.5 1.9 collective-permute-start.12
  57.4 6.0 %collective-permute-start.13 = (f32[12,3,16,2]{3,0,2,1:T(8,128)S(1)}, f32[12,3,16,2]{3,0,2,1:T(8,128)S(1)}, u32[]{:S(2)}, u32[]{:S(2)}) collective-permute-start(f32[12,3,16,2]{3,0,2,1:T(8,128)S(1)} %get-tuple-element.59), channel_id=1, source_target_pairs={{16,0},{32,16},{48,32},{64,48},{80,64},{96,80},{112,96},{128,112},... | collective-permute-start | bytes 13832 | tf_op jit(solution)/shard_map/ppermute | solution.py:33
  63.4 1.2 collective-permute-done.12
  64.9 3.8 %collective-permute-start.14 = (f32[12,3,2,132]{3,0,2,1:T(8,128)S(1)}, f32[12,3,2,132]{3,0,2,1:T(8,128)S(1)}, u32[]{:S(2)}, u32[]{:S(2)}) collective-permute-start(f32[12,3,2,132]{3,0,2,1:T(8,128)S(1)} %get-tuple-element.10), channel_id=1, source_target_pairs={{0,1},{1,2},{2,3},{3,4},{4,5},{5,6},{6,7},{7,8},{8,9},{9,10},{10,1... | collective-permute-start | bytes 114056 | tf_op jit(solution)/shard_map/ppermute | solution.py:30
  68.7 1.5 collective-permute-start.15
  70.3 4.0 %collective-permute-done.15 = f32[12,3,2,132]{3,0,2,1:T(8,128)S(1)} collective-permute-done((f32[12,3,2,132]{3,0,2,1:T(8,128)S(1)}, f32[12,3,2,132]{3,0,2,1:T(8,128)S(1)}, u32[]{:S(2)}, u32[]{:S(2)}) %collective-permute-start.15) | collective-permute-done | bytes 38048 | tf_op jit(solution)/shard_map/ppermute | solution.py:33
  74.3 0.4 pad_maximum_fusion.2
  74.9 0.6 add_bitcast_fusion.3
  75.5 0.6 add_bitcast_fusion.2
  76.1 0.6 fusion.13
  77.3 0.3 add_bitcast_fusion.10
  77.7 0.3 fusion.33
  78.2 1.0 collective-permute-start.16
  79.2 7.2 %collective-permute-start.17 = (f32[12,3,16,2]{3,0,2,1:T(8,128)S(1)}, f32[12,3,16,2]{3,0,2,1:T(8,128)S(1)}, u32[]{:S(2)}, u32[]{:S(2)}) collective-permute-start(f32[12,3,16,2]{3,0,2,1:T(8,128)S(1)} %get-tuple-element.57), channel_id=1, source_target_pairs={{16,0},{32,16},{48,32},{64,48},{80,64},{96,80},{112,96},{128,112},... | collective-permute-start | bytes 13832 | tf_op jit(solution)/shard_map/ppermute | solution.py:33
  86.4 1.2 collective-permute-done.16
  87.9 3.8 %collective-permute-start.18 = (f32[12,3,2,132]{3,0,2,1:T(8,128)S(1)}, f32[12,3,2,132]{3,0,2,1:T(8,128)S(1)}, u32[]{:S(2)}, u32[]{:S(2)}) collective-permute-start(f32[12,3,2,132]{3,0,2,1:T(8,128)S(1)} %get-tuple-element.8), channel_id=1, source_target_pairs={{0,1},{1,2},{2,3},{3,4},{4,5},{5,6},{6,7},{7,8},{8,9},{9,10},{10,1... | collective-permute-start | bytes 114056 | tf_op jit(solution)/shard_map/ppermute | solution.py:30
  91.7 1.3 collective-permute-start.19
  93.0 0.3 collective-permute-done.18
  93.3 4.0 %collective-permute-done.19 = f32[12,3,2,132]{3,0,2,1:T(8,128)S(1)} collective-permute-done((f32[12,3,2,132]{3,0,2,1:T(8,128)S(1)}, f32[12,3,2,132]{3,0,2,1:T(8,128)S(1)}, u32[]{:S(2)}, u32[]{:S(2)}) %collective-permute-start.19) | collective-permute-done | bytes 38048 | tf_op jit(solution)/shard_map/ppermute | solution.py:33
  97.3 0.4 pad_maximum_fusion.3
  97.9 0.6 add_bitcast_fusion.1
  98.5 0.6 add_bitcast_fusion
  99.1 0.6 fusion.8
  100.4 0.3 add_bitcast_fusion.8
  101.0 0.6 fusion.1
  101.8 261.1 %all-gather.1 = f32[512,12,12]{2,1,0:T(8,128)} all-gather(f32[1,12,12]{2,1,0:T(8,128)S(1)} %fusion.1), channel_id=2, replica_groups=mesh['lon'=32,'lat'=16] {'lon','lat'}, dimensions={0}, use_global_device_ids=true | all-gather | bytes 295488 | tf_op jit(solution)/shard_map/all_gather | solution.py:17
  362.9 2.7 reduce_sum.9
  365.8 1.1 cholesky.16
  366.9 0.6 compare_reduce_fusion
  367.5 0.6 fusion.54
  368.2 0.7 copy.29
  368.9 0.9 custom-call.7
  369.8 0.6 fusion.2
  370.4 0.8 copy.28
  (63 shorter events, 6.7 us)
Async XLA Ops:
  1.4 11.8 %collective-permute-start.4 = (f32[1,3,16,2]{3,2,1,0:T(8,128)S(1)}, f32[1,3,16,2]{3,2,1,0:T(8,128)S(1)}, u32[]{:S(2)}, u32[]{:S(2)}) collective-permute-start(f32[1,3,16,2]{3,2,1,0:T(8,128)S(1)} %get-tuple-element.84), channel_id=1, source_target_pairs={{0,16},{16,32},{32,48},{48,64},{64,80},{80,96},{96,112},{112,128},... | collective-permute-start | bytes 1160 | tf_op jit(solution)/shard_map/ppermute | solution.py:30
  4.5 8.8 %collective-permute-start.5 = (f32[1,3,16,2]{3,2,1,0:T(8,128)S(1)}, f32[1,3,16,2]{3,2,1,0:T(8,128)S(1)}, u32[]{:S(2)}, u32[]{:S(2)}) collective-permute-start(f32[1,3,16,2]{3,2,1,0:T(8,128)S(1)} %get-tuple-element.85), channel_id=1, source_target_pairs={{16,0},{32,16},{48,32},{64,48},{80,64},{96,80},{112,96},{128,112},... | collective-permute-start | bytes 1160 | tf_op jit(solution)/shard_map/ppermute | solution.py:33
  9.5 12.1 %collective-permute-start = (f32[12,3,16,2]{3,0,2,1:T(8,128)S(1)}, f32[12,3,16,2]{3,0,2,1:T(8,128)S(1)}, u32[]{:S(2)}, u32[]{:S(2)}) collective-permute-start(f32[12,3,16,2]{3,0,2,1:T(8,128)S(1)} %get-tuple-element.62), channel_id=1, source_target_pairs={{0,16},{16,32},{32,48},{48,64},{64,80},{80,96},{96,112},{112,128},... | collective-permute-start | bytes 13832 | tf_op jit(solution)/shard_map/ppermute | solution.py:30
  9.6 12.0 %collective-permute-start.1 = (f32[12,3,16,2]{3,0,2,1:T(8,128)S(1)}, f32[12,3,16,2]{3,0,2,1:T(8,128)S(1)}, u32[]{:S(2)}, u32[]{:S(2)}) collective-permute-start(f32[12,3,16,2]{3,0,2,1:T(8,128)S(1)} %get-tuple-element.63), channel_id=1, source_target_pairs={{16,0},{32,16},{48,32},{64,48},{80,64},{96,80},{112,96},{128,112},... | collective-permute-start | bytes 13832 | tf_op jit(solution)/shard_map/ppermute | solution.py:33
  13.4 4.4 %collective-permute-start.6 = (f32[1,3,2,132]{3,2,1,0:T(2,128)S(1)}, f32[1,3,2,132]{3,2,1,0:T(2,128)S(1)}, u32[]{:S(2)}, u32[]{:S(2)}) collective-permute-start(f32[1,3,2,132]{3,2,1,0:T(2,128)S(1)} %get-tuple-element.70), channel_id=1, source_target_pairs={{0,1},{1,2},{2,3},{3,4},{4,5},{5,6},{6,7},{7,8},{8,9},{9,10},{10,1... | collective-permute-start | bytes 9512 | tf_op jit(solution)/shard_map/ppermute | solution.py:30
  16.5 4.7 %collective-permute-start.7 = (f32[1,3,2,132]{3,2,1,0:T(2,128)S(1)}, f32[1,3,2,132]{3,2,1,0:T(2,128)S(1)}, u32[]{:S(2)}, u32[]{:S(2)}) collective-permute-start(f32[1,3,2,132]{3,2,1,0:T(2,128)S(1)} %get-tuple-element.71), channel_id=1, source_target_pairs={{1,0},{2,1},{3,2},{4,3},{5,4},{6,5},{7,6},{8,7},{9,8},{10,9},{11,1... | collective-permute-start | bytes 9512 | tf_op jit(solution)/shard_map/ppermute | solution.py:33
  21.7 4.7 %collective-permute-start.2 = (f32[12,3,2,132]{3,0,2,1:T(8,128)S(1)}, f32[12,3,2,132]{3,0,2,1:T(8,128)S(1)}, u32[]{:S(2)}, u32[]{:S(2)}) collective-permute-start(f32[12,3,2,132]{3,0,2,1:T(8,128)S(1)} %get-tuple-element.14), channel_id=1, source_target_pairs={{0,1},{1,2},{2,3},{3,4},{4,5},{5,6},{6,7},{7,8},{8,9},{9,10},{10,1... | collective-permute-start | bytes 114056 | tf_op jit(solution)/shard_map/ppermute | solution.py:30
  24.9 5.4 %collective-permute-start.3 = (f32[12,3,2,132]{3,0,2,1:T(8,128)S(1)}, f32[12,3,2,132]{3,0,2,1:T(8,128)S(1)}, u32[]{:S(2)}, u32[]{:S(2)}) collective-permute-start(f32[12,3,2,132]{3,0,2,1:T(8,128)S(1)} %get-tuple-element.15), channel_id=1, source_target_pairs={{1,0},{2,1},{3,2},{4,3},{5,4},{6,5},{7,6},{8,7},{9,8},{10,9},{11,1... | collective-permute-start | bytes 114056 | tf_op jit(solution)/shard_map/ppermute | solution.py:33
  34.1 6.7 %collective-permute-start.8 = (f32[12,3,16,2]{3,0,2,1:T(8,128)S(1)}, f32[12,3,16,2]{3,0,2,1:T(8,128)S(1)}, u32[]{:S(2)}, u32[]{:S(2)}) collective-permute-start(f32[12,3,16,2]{3,0,2,1:T(8,128)S(1)} %get-tuple-element.60), channel_id=1, source_target_pairs={{0,16},{16,32},{32,48},{48,64},{64,80},{80,96},{96,112},{112,128},... | collective-permute-start | bytes 13832 | tf_op jit(solution)/shard_map/ppermute | solution.py:30
  34.2 7.2 %collective-permute-start.9 = (f32[12,3,16,2]{3,0,2,1:T(8,128)S(1)}, f32[12,3,16,2]{3,0,2,1:T(8,128)S(1)}, u32[]{:S(2)}, u32[]{:S(2)}) collective-permute-start(f32[12,3,16,2]{3,0,2,1:T(8,128)S(1)} %get-tuple-element.61), channel_id=1, source_target_pairs={{16,0},{32,16},{48,32},{64,48},{80,64},{96,80},{112,96},{128,112},... | collective-permute-start | bytes 13832 | tf_op jit(solution)/shard_map/ppermute | solution.py:33
  41.5 6.3 %collective-permute-start.10 = (f32[12,3,2,132]{3,0,2,1:T(8,128)S(1)}, f32[12,3,2,132]{3,0,2,1:T(8,128)S(1)}, u32[]{:S(2)}, u32[]{:S(2)}) collective-permute-start(f32[12,3,2,132]{3,0,2,1:T(8,128)S(1)} %get-tuple-element.12), channel_id=1, source_target_pairs={{0,1},{1,2},{2,3},{3,4},{4,5},{5,6},{6,7},{7,8},{8,9},{9,10},{10,1... | collective-permute-start | bytes 114056 | tf_op jit(solution)/shard_map/ppermute | solution.py:30
  46.3 5.4 %collective-permute-start.11 = (f32[12,3,2,132]{3,0,2,1:T(8,128)S(1)}, f32[12,3,2,132]{3,0,2,1:T(8,128)S(1)}, u32[]{:S(2)}, u32[]{:S(2)}) collective-permute-start(f32[12,3,2,132]{3,0,2,1:T(8,128)S(1)} %get-tuple-element.13), channel_id=1, source_target_pairs={{1,0},{2,1},{3,2},{4,3},{5,4},{6,5},{7,6},{8,7},{9,8},{10,9},{11,1... | collective-permute-start | bytes 114056 | tf_op jit(solution)/shard_map/ppermute | solution.py:33
  55.5 9.1 %collective-permute-start.12 = (f32[12,3,16,2]{3,0,2,1:T(8,128)S(1)}, f32[12,3,16,2]{3,0,2,1:T(8,128)S(1)}, u32[]{:S(2)}, u32[]{:S(2)}) collective-permute-start(f32[12,3,16,2]{3,0,2,1:T(8,128)S(1)} %get-tuple-element.58), channel_id=1, source_target_pairs={{0,16},{16,32},{32,48},{48,64},{64,80},{80,96},{96,112},{112,128},... | collective-permute-start | bytes 13832 | tf_op jit(solution)/shard_map/ppermute | solution.py:30
  57.4 7.4 %collective-permute-start.13 = (f32[12,3,16,2]{3,0,2,1:T(8,128)S(1)}, f32[12,3,16,2]{3,0,2,1:T(8,128)S(1)}, u32[]{:S(2)}, u32[]{:S(2)}) collective-permute-start(f32[12,3,16,2]{3,0,2,1:T(8,128)S(1)} %get-tuple-element.59), channel_id=1, source_target_pairs={{16,0},{32,16},{48,32},{64,48},{80,64},{96,80},{112,96},{128,112},... | collective-permute-start | bytes 13832 | tf_op jit(solution)/shard_map/ppermute | solution.py:33
  64.9 5.4 %collective-permute-start.14 = (f32[12,3,2,132]{3,0,2,1:T(8,128)S(1)}, f32[12,3,2,132]{3,0,2,1:T(8,128)S(1)}, u32[]{:S(2)}, u32[]{:S(2)}) collective-permute-start(f32[12,3,2,132]{3,0,2,1:T(8,128)S(1)} %get-tuple-element.10), channel_id=1, source_target_pairs={{0,1},{1,2},{2,3},{3,4},{4,5},{5,6},{6,7},{7,8},{8,9},{9,10},{10,1... | collective-permute-start | bytes 114056 | tf_op jit(solution)/shard_map/ppermute | solution.py:30
  68.7 5.6 %collective-permute-start.15 = (f32[12,3,2,132]{3,0,2,1:T(8,128)S(1)}, f32[12,3,2,132]{3,0,2,1:T(8,128)S(1)}, u32[]{:S(2)}, u32[]{:S(2)}) collective-permute-start(f32[12,3,2,132]{3,0,2,1:T(8,128)S(1)} %get-tuple-element.11), channel_id=1, source_target_pairs={{1,0},{2,1},{3,2},{4,3},{5,4},{6,5},{7,6},{8,7},{9,8},{10,9},{11,1... | collective-permute-start | bytes 114056 | tf_op jit(solution)/shard_map/ppermute | solution.py:33
  78.2 9.4 %collective-permute-start.16 = (f32[12,3,16,2]{3,0,2,1:T(8,128)S(1)}, f32[12,3,16,2]{3,0,2,1:T(8,128)S(1)}, u32[]{:S(2)}, u32[]{:S(2)}) collective-permute-start(f32[12,3,16,2]{3,0,2,1:T(8,128)S(1)} %get-tuple-element.56), channel_id=1, source_target_pairs={{0,16},{16,32},{32,48},{48,64},{64,80},{80,96},{96,112},{112,128},... | collective-permute-start | bytes 13832 | tf_op jit(solution)/shard_map/ppermute | solution.py:30
  79.2 8.6 %collective-permute-start.17 = (f32[12,3,16,2]{3,0,2,1:T(8,128)S(1)}, f32[12,3,16,2]{3,0,2,1:T(8,128)S(1)}, u32[]{:S(2)}, u32[]{:S(2)}) collective-permute-start(f32[12,3,16,2]{3,0,2,1:T(8,128)S(1)} %get-tuple-element.57), channel_id=1, source_target_pairs={{16,0},{32,16},{48,32},{64,48},{80,64},{96,80},{112,96},{128,112},... | collective-permute-start | bytes 13832 | tf_op jit(solution)/shard_map/ppermute | solution.py:33
  87.9 5.4 %collective-permute-start.18 = (f32[12,3,2,132]{3,0,2,1:T(8,128)S(1)}, f32[12,3,2,132]{3,0,2,1:T(8,128)S(1)}, u32[]{:S(2)}, u32[]{:S(2)}) collective-permute-start(f32[12,3,2,132]{3,0,2,1:T(8,128)S(1)} %get-tuple-element.8), channel_id=1, source_target_pairs={{0,1},{1,2},{2,3},{3,4},{4,5},{5,6},{6,7},{7,8},{8,9},{9,10},{10,1... | collective-permute-start | bytes 114056 | tf_op jit(solution)/shard_map/ppermute | solution.py:30
  91.7 5.6 %collective-permute-start.19 = (f32[12,3,2,132]{3,0,2,1:T(8,128)S(1)}, f32[12,3,2,132]{3,0,2,1:T(8,128)S(1)}, u32[]{:S(2)}, u32[]{:S(2)}) collective-permute-start(f32[12,3,2,132]{3,0,2,1:T(8,128)S(1)} %get-tuple-element.9), channel_id=1, source_target_pairs={{1,0},{2,1},{3,2},{4,3},{5,4},{6,5},{7,6},{8,7},{9,8},{10,9},{11,1... | collective-permute-start | bytes 114056 | tf_op jit(solution)/shard_map/ppermute | solution.py:33
